TPU v7x, 512 devices: a whole 4x4x16 slice. The times are simulated.
512 devices in a mesh: section: 2 (over x_hi), lat: 64 (over z, x_lo, core), tp: 4 (over y).
Axes of the slice: x: 4 (x_hi: 2, x_lo: 2; x = x_hi * 2 + x_lo), y: 4, z: 16, core: 2. Of those that a mesh axis runs over, the one named last changes fastest.
Arguments:
- initial_field: bfloat16 [2, 8, 192, 48, 192], P(None, 'tp', 'lat'), may hold values from -6 to 6
- first_gain: bfloat16 [2, 192], P('section'), may hold values from 0.25 to 1.75
- first_shift: bfloat16 [2, 192], P('section'), may hold values from -1.75 to 1.75
- qkv_weight: bfloat16 [2, 192, 576], P('section', None, 'tp'), may hold values from -0.4375 to 0.4375
- qkv_bias: bfloat16 [2, 576], P('section', 'tp'), may hold values from -1.75 to 1.75
- proj_weight: bfloat16 [2, 192, 192], P('section', None, 'tp'), may hold values from -0.4375 to 0.4375
- proj_bias: bfloat16 [2, 192], P('section', 'tp'), may hold values from -1.75 to 1.75
- second_gain: bfloat16 [2, 192], P('section'), may hold values from 0.25 to 1.75
- second_shift: bfloat16 [2, 192], P('section'), may hold values from -1.75 to 1.75
- expand_weight: bfloat16 [2, 192, 768], P('section', None, 'tp'), may hold values from -0.4375 to 0.4375
- expand_bias: bfloat16 [2, 768], P('section', 'tp'), may hold values from -1.75 to 1.75
- reduce_weight: bfloat16 [2, 768, 192], P('section', 'tp'), may hold values from -0.21875 to 0.21875
- reduce_bias: bfloat16 [2, 192], P('section', 'tp'), may hold values from -1.75 to 1.75
- earth_bias: float32 [2, 4, 64, 6, 1656], P('section', 'tp', 'lat'), may hold values from -4 to 340
Outputs:
- predicted_states: bfloat16 [2, 2, 8, 192, 48, 192], P('section', None, 'tp', 'lat')
All inputs are finite; a program needn't handle non-finite values.
Results may differ from a plain program's by a relative error of at most 0.018.
Values may be sent and summed in bfloat16 or wider, within the bound.
No kernel may reach another device: no remote copies, remote signals or barrier semaphores. Data moves between devices by JAX's collectives and lax.ppermute only.
A program may use at most 64 MiB of HBM per device.

v0:
```python
import jax
import jax.numpy as jnp
import numpy as np
from jax import lax
from jax.sharding import PartitionSpec as P

WZ = 2
WH = 6
WW = 12
epsilon = 1e-05


def swapped(block, axis, apart):
    count = lax.axis_size(axis)
    route = []
    for low in range(count):
        high = low | 1 << apart
        if high != low and high < count:
            route += [(low, high), (high, low)]
    return lax.ppermute(block, axis, route)


def passed_along(value, axis, steps):
    count = lax.axis_size(axis)
    first, last = (max(0, -steps), min(count, count - steps))
    return lax.ppermute(value, axis, [(source, source + steps) for source in range(first, last)])


def bias_entries():
    half_rows = WH // 2
    query_pos = np.arange(WZ * half_rows * WW)
    attended_location = np.arange(WZ * WH * WW)
    query_level = query_pos // (half_rows * WW)
    query_row = query_pos // WW % half_rows
    query_col = query_pos % WW
    key_level = attended_location // (WH * WW)
    key_row = attended_location // WW % WH
    key_column_index = attended_location % WW
    table_items = (
        ((query_level[:, None] * WZ + key_level[None, :]) * half_rows + query_row[:, None]) * WH
        + key_row[None, :]
    ) * (2 * WW - 1) + (query_col[:, None] - key_column_index[None, :] + WW - 1)
    return table_items.astype(np.int32)


def layer_norm(values, gain, offset):
    floats = values.astype(jnp.float32)
    middle_point = jnp.mean(floats, axis=-1, keepdims=True)
    spread = jnp.mean((floats - middle_point) ** 2, axis=-1, keepdims=True)
    return (floats - middle_point) * lax.rsqrt(spread + epsilon) * gain.astype(
        jnp.float32
    ) + offset.astype(jnp.float32)


def earth_block(grid, norms, weights, bias_block, band_half):
    first_gain, first_shift, second_gain, second_shift = norms
    (
        qkv_matrix,
        qkv_offset,
        proj_matrix,
        proj_offset,
        expand_matrix,
        expand_offset,
        reduce_matrix,
        shrink_translation,
    ) = weights
    levels, lat_rows, lon_cols, width = grid.shape
    heads = bias_block.shape[0]
    head_size = width // heads
    scale = 1.0 / float(np.sqrt(head_size))
    meridian_slabs = lon_cols // WW
    normed = layer_norm(grid, first_gain, first_shift).astype(jnp.bfloat16)
    flat = normed.reshape(-1, width)
    own_mixed = (
        jnp.dot(flat, qkv_matrix, preferred_element_type=jnp.float32)
        + qkv_offset.astype(jnp.float32)
    ).astype(jnp.bfloat16)
    neighbour_keyvalue = swapped(own_mixed[:, width:], "lat", 0)
    own_kv = own_mixed[:, width:].reshape(levels, lat_rows, lon_cols, 2 * width)
    neighbour_keyvalue = neighbour_keyvalue.reshape(levels, lat_rows, lon_cols, 2 * width)
    lower_first = jnp.concatenate([own_kv, neighbour_keyvalue], axis=1)
    upper_first = jnp.concatenate([neighbour_keyvalue, own_kv], axis=1)
    window_kv = jnp.where(band_half == 0, lower_first, upper_first)
    keyvals = window_kv.reshape(levels, 2 * lat_rows, meridian_slabs, WW, 2 * width).transpose(
        2, 0, 1, 3, 4
    )
    keyvals = keyvals.reshape(meridian_slabs, levels * 2 * lat_rows * WW, 2 * width)
    query_rows = (
        own_mixed[:, :width]
        .reshape(levels, lat_rows, meridian_slabs, WW, width)
        .transpose(2, 0, 1, 3, 4)
    )
    query_rows = query_rows.reshape(meridian_slabs, levels * lat_rows * WW, width)
    query_count = query_rows.shape[1]
    key_count = keyvals.shape[1]
    query_heads = query_rows.reshape(meridian_slabs, query_count, heads, head_size)
    key_heads = keyvals[..., :width].reshape(meridian_slabs, key_count, heads, head_size)
    value_heads = keyvals[..., width:].reshape(meridian_slabs, key_count, heads, head_size)
    scores = (
        jnp.einsum("wqhd,wkhd->whqk", query_heads, key_heads, preferred_element_type=jnp.float32)
        * scale
        + bias_block[None]
    )
    probs = jax.nn.softmax(scores, axis=-1).astype(jnp.bfloat16)
    attended = jnp.einsum(
        "whqk,wkhd->wqhd", probs, value_heads, preferred_element_type=jnp.float32
    ).astype(jnp.bfloat16)
    merged = (
        attended.reshape(meridian_slabs, levels, lat_rows, WW, width)
        .transpose(1, 2, 0, 3, 4)
        .reshape(-1, width)
    )
    branch = jnp.dot(merged, proj_matrix, preferred_element_type=jnp.float32) + proj_offset.astype(
        jnp.float32
    )
    middle = (grid.reshape(-1, width).astype(jnp.float32) + branch).astype(jnp.bfloat16)
    normed_two = layer_norm(middle, second_gain, second_shift).astype(jnp.bfloat16)
    hidden = jax.nn.gelu(
        jnp.dot(normed_two, expand_matrix, preferred_element_type=jnp.float32)
        + expand_offset.astype(jnp.float32),
        approximate=False,
    ).astype(jnp.bfloat16)
    result = (
        middle.astype(jnp.float32)
        + jnp.dot(hidden, reduce_matrix, preferred_element_type=jnp.float32)
        + shrink_translation.astype(jnp.float32)
    ).astype(jnp.bfloat16)
    return result.reshape(levels, lat_rows, lon_cols, width)


def on_device(
    initial_field,
    first_gain,
    first_shift,
    qkv_weight,
    qkv_bias,
    proj_weight,
    proj_bias,
    second_gain,
    second_shift,
    expand_weight,
    expand_bias,
    reduce_weight,
    reduce_bias,
    earth_bias,
):
    collected_values = (
        lax.all_gather(qkv_weight, "tp", axis=2, tiled=True),
        lax.all_gather(qkv_bias, "tp", axis=1, tiled=True),
        lax.all_gather(proj_weight, "tp", axis=2, tiled=True),
        lax.all_gather(proj_bias, "tp", axis=1, tiled=True),
        lax.all_gather(expand_weight, "tp", axis=2, tiled=True),
        lax.all_gather(expand_bias, "tp", axis=1, tiled=True),
        lax.all_gather(reduce_weight, "tp", axis=1, tiled=True),
        lax.all_gather(reduce_bias, "tp", axis=1, tiled=True),
    )
    weights = tuple((piece[0] for piece in collected_values))
    norms = (first_gain[0], first_shift[0], second_gain[0], second_shift[0])
    bias_table = earth_bias[0, 0, 0]
    table_items = jnp.asarray(bias_entries())
    portion_index = lax.axis_index("section")
    band_half = lax.axis_index("lat") % 2
    micro_count = initial_field.shape[0]
    bias_block = jnp.take(bias_table, table_items, axis=1)
    carried = jnp.zeros_like(initial_field[0])
    daily_lead_times = []
    quarter_lead_times = []
    for turn_index in range(micro_count + 1):
        own_field = initial_field[min(turn_index, micro_count - 1)]
        block_input = jnp.where(portion_index == 0, own_field, carried)
        block_output = earth_block(block_input, norms, weights, bias_block, band_half)
        if turn_index < micro_count:
            daily_lead_times.append(block_output)
            carried = passed_along(block_output, "section", 1)
        if turn_index > 0:
            quarter_lead_times.append(block_output)
    predicted_states = jnp.where(
        portion_index == 0, jnp.stack(daily_lead_times), jnp.stack(quarter_lead_times)
    )
    return predicted_states[None]


def solution(mesh):
    return jax.shard_map(
        on_device,
        mesh=mesh,
        in_specs=(
            P(None, "tp", "lat", None, None),
            P("section", None),
            P("section", None),
            P("section", None, "tp"),
            P("section", "tp"),
            P("section", None, "tp"),
            P("section", "tp"),
            P("section", None),
            P("section", None),
            P("section", None, "tp"),
            P("section", "tp"),
            P("section", "tp", None),
            P("section", "tp"),
            P("section", "tp", "lat", None, None),
        ),
        out_specs=P("section", None, "tp", "lat", None, None),
        check_vma=False,
    )
```

profile of v0, /device:TPU:455, one launch (start us, length us, event | category | flops | bytes accessed | tf_op | source)
XLA Modules:
  0.0 165.5 jit_solution(211439283647402022)
XLA Ops:
  1.0 1.1 fusion.184
  3.5 1.3 dynamic-slice
  10.3 8.8 %all-reduce.4 = (bf16[768]{0:T(1024)(128)(2,1)S(1)}, bf16[192]{0:T(256)(128)(2,1)S(1)}, bf16[576]{0:T(1024)(128)(2,1)S(1)}, bf16[192]{0:T(256)(128)(2,1)S(1)}) all-reduce(bf16[768]{0:T(1024)(128)(2,1)S(1)} %dynamic-update-slice.2, bf16[192]{0:T(256)(128)(2,1)S(1)} %dynamic-update-slice.1, ...), channel_id=1, replica_groups=mesh['section'=2,'lat'=64,'tp'=4] {'tp'}, use_global_device_ids=true, to_apply=%add.2 | all-reduce | flops 1728 | bytes 6912
  19.1 10.2 %all_gather.24 = bf16[1,192,576]{1,2,0:T(8,128)(2,1)S(1)} all-gather(bf16[1,192,144]{1,2,0:T(8,128)(2,1)} %param.18), channel_id=1, replica_groups=mesh['section'=2,'lat'=64,'tp'=4] {'tp'}, dimensions={2}, use_global_device_ids=true | all-gather | bytes 276480 | tf_op jit(solution)/shard_map/all_gather | solution.py:148
  30.9 6.9 %collective-permute-start = (bf16[288,384]{1,0:T(8,128)(2,1)S(1)}, bf16[288,384]{1,0:T(8,128)(2,1)}, u32[]{:S(2)}, u32[]{:S(2)}) collective-permute-start(bf16[288,384]{1,0:T(8,128)(2,1)S(1)} %slice.62), channel_id=1, source_target_pairs={{0,4},{4,0},{8,12},{12,8},{16,20},{20,16},{24,28},{28,24},{32,36},... | collective-permute-start | bytes 663560 | tf_op jit(solution)/shard_map/ppermute | solution.py:20
  38.7 19.9 %gather_fusion = f32[10368,6]{1,0:T(8,128)} fusion(f32[6,1656]{0,1:T(8,128)S(1)} %bitcast.127, s32[11264]{0:T(1024)S(1)} %pad_clamp_fusion), kind=kCustom, calls=%fused_computation | custom fusion | bytes 539136 | tf_op jit(solution)/shard_map/jit(_take)/gather | solution.py:164
  58.6 4.8 %copy.74 = f32[72,144,6]{1,0,2:T(8,128)S(1)} copy(f32[72,144,6]{2,1,0:T(8,128)} %bitcast.128) | data formatting | bytes 497664 | tf_op jit(solution)/shard_map/jit(_take)/gather | solution.py:164
  63.5 9.2 %all_gather.26 = bf16[1,192,192]{1,2,0:T(8,128)(2,1)S(1)} all-gather(bf16[1,192,48]{1,2,0:T(8,128)(2,1)S(1)} %copy-done.10), channel_id=1, replica_groups=mesh['section'=2,'lat'=64,'tp'=4] {'tp'}, dimensions={2}, use_global_device_ids=true | all-gather | bytes 92160 | tf_op jit(solution)/shard_map/all_gather | solution.py:150
  74.0 12.2 %all_gather.28 = bf16[1,192,768]{1,0,2:T(2,128)(2,1)S(1)} all-gather(bf16[1,192,192]{1,0,2:T(2,128)(2,1)S(1)} %copy.77), channel_id=1, replica_groups=mesh['section'=2,'lat'=64,'tp'=4] {'tp'}, dimensions={2}, use_global_device_ids=true | all-gather | bytes 368640 | tf_op jit(solution)/shard_map/all_gather | solution.py:152
  86.6 10.6 %all_gather.30 = bf16[1,768,192]{2,1,0:T(8,128)(2,1)} all-gather(bf16[1,192,192]{2,1,0:T(8,128)(2,1)} %param.26), channel_id=1, replica_groups=mesh['section'=2,'lat'=64,'tp'=4] {'tp'}, dimensions={1}, use_global_device_ids=true | all-gather | bytes 368640 | tf_op jit(solution)/shard_map/all_gather | solution.py:154
  100.6 3.8 %fusion.18 = bf16[4,72,6,32]{1,3,2,0:T(8,128)(2,1)} fusion(bf16[4,144,6,32]{1,3,2,0:T(8,128)(2,1)S(1)} %bitcast.155, f32[4,6,72]{2,1,0:T(8,128)S(1)} %fusion.354, f32[6,72,144]{2,1,0:T(8,128)S(1)} %bitcast.143, bf16[4,144,6,32]{1,3,2,0:T(8,128)(2,1)S(1)} %bitcast.151, bf16[4,72,6,32]{3,2,0,1:T(8,128)(2,1)S(1)} %reshape_reshape.9), kind=kOutput, calls=%fused_computation.46 | convolution fusion | flops 33151824 | bytes 919296 | tf_op jit(solution)/shard_map/whqk,wkhd->wqhd/dot_general | solution.py:105
  104.4 1.8 %copy.75 = bf16[4,72,6,32]{3,2,0,1:T(8,128)(2,1)S(1)} copy(bf16[4,72,6,32]{1,3,2,0:T(8,128)(2,1)} %fusion.18) | data formatting | bytes 221184 | tf_op jit(solution)/shard_map/convert_element_type | solution.py:107
  107.3 2.4 %fusion.17 = bf16[288,192]{1,0:T(8,128)(2,1)S(1)} fusion(f32[288,192]{1,0:T(8,128)S(1)} %get-tuple-element.20, f32[768]{0:T(1024)S(1)} %copy-done.11, bf16[1,768,192]{2,1,0:T(8,128)(2,1)S(1)} %copy-done.1, bf16[1,192,768]{2,1,0:T(8,128)(2,1)S(1)} %copy.78, f32[192]{0:T(256)S(1)} %copy-done.22, f32[192]{0:T(256)S(1)} %bitcast.171, f32[192]{0:T(256)S(1)} %bitcast.168, ...), kind=kOutput, calls=%fused_computation.45 | convolution fusion | flops 184909824 | bytes 929280 | tf_op jit(solution)/shard_map/dot_general | solution.py:125
  109.7 1.5 collective-permute-start.1
  111.2 5.9 %collective-permute-done.1 = bf16[2,3,48,192]{3,2,1,0:T(8,128)(2,1)S(1)} collective-permute-done((bf16[2,3,48,192]{3,2,1,0:T(8,128)(2,1)S(1)}, bf16[2,3,48,192]{3,2,1,0:T(8,128)(2,1)S(1)}, u32[]{:S(2)}, u32[]{:S(2)}) %collective-permute-start.1) | collective-permute-done | bytes 110624 | tf_op jit(solution)/shard_map/ppermute | solution.py:26
  118.1 10.0 %collective-permute-start.2 = (bf16[288,384]{1,0:T(8,128)(2,1)S(1)}, bf16[288,384]{1,0:T(8,128)(2,1)S(1)}, u32[]{:S(2)}, u32[]{:S(2)}) collective-permute-start(bf16[288,384]{1,0:T(8,128)(2,1)S(1)} %slice.66), channel_id=1, source_target_pairs={{0,4},{4,0},{8,12},{12,8},{16,20},{20,16},{24,28},{28,24},{32,36},... | collective-permute-start | bytes 663560 | tf_op jit(solution)/shard_map/ppermute | solution.py:20
  131.2 1.7 %fusion.358 = f32[4,6,72]{2,1,0:T(8,128)} fusion(f32[6,72,144]{2,1,0:T(8,128)S(1)} %bitcast.144, bf16[4,144,6,32]{1,3,2,0:T(8,128)(2,1)S(1)} %bitcast.152, bf16[4,72,6,32]{3,2,0,1:T(8,128)(2,1)S(1)} %reshape_reshape.10), kind=kOutput, calls=%fused_computation.393 | convolution fusion | flops 16920720 | bytes 587520 | tf_op jit(solution)/shard_map/sub | solution.py:104
  132.9 3.9 %fusion.19 = bf16[4,72,6,32]{1,3,2,0:T(8,128)(2,1)S(1)} fusion(bf16[4,144,6,32]{1,3,2,0:T(8,128)(2,1)S(1)} %bitcast.156, f32[4,6,72]{2,1,0:T(8,128)} %fusion.358, f32[6,72,144]{2,1,0:T(8,128)S(1)} %bitcast.145, bf16[4,144,6,32]{1,3,2,0:T(8,128)(2,1)S(1)} %bitcast.153, bf16[4,72,6,32]{3,2,0,1:T(8,128)(2,1)S(1)} %reshape_reshape.10), kind=kOutput, calls=%fused_computation.47 | convolution fusion | flops 33151824 | bytes 919296 | tf_op jit(solution)/shard_map/whqk,wkhd->wqhd/dot_general | solution.py:105
  138.8 2.4 %fusion.16 = bf16[288,192]{1,0:T(8,128)(2,1)S(1)} fusion(f32[768]{0:T(1024)S(1)} %copy-done.12, bf16[288,192]{1,0:T(8,128)(2,1)S(1)} %fusion.189, bf16[1,768,192]{2,1,0:T(8,128)(2,1)S(1)} %copy-done.1, bf16[1,192,768]{2,1,0:T(8,128)(2,1)S(1)} %copy.78, f32[192]{0:T(256)S(1)} %copy-done.23, f32[288]{0:T(512)S(1)} %add_rsqrt_fusion.4, ...), kind=kOutput, calls=%fused_computation.44 | convolution fusion | flops 185020416 | bytes 818688 | tf_op jit(solution)/shard_map/dot_general | solution.py:125
  141.2 1.3 collective-permute-start.3
  142.5 7.2 %collective-permute-done.3 = bf16[2,3,48,192]{3,2,1,0:T(8,128)(2,1)S(1)} collective-permute-done((bf16[2,3,48,192]{3,2,1,0:T(8,128)(2,1)S(1)}, bf16[2,3,48,192]{3,2,1,0:T(8,128)(2,1)S(1)}, u32[]{:S(2)}, u32[]{:S(2)}) %collective-permute-start.3) | collective-permute-done | bytes 110624 | tf_op jit(solution)/shard_map/ppermute | solution.py:26
  150.6 3.3 %collective-permute-start.4 = (bf16[288,384]{1,0:T(8,128)(2,1)S(1)}, bf16[288,384]{1,0:T(8,128)(2,1)S(1)}, u32[]{:S(2)}, u32[]{:S(2)}) collective-permute-start(bf16[288,384]{1,0:T(8,128)(2,1)S(1)} %slice.70), channel_id=1, source_target_pairs={{0,4},{4,0},{8,12},{12,8},{16,20},{20,16},{24,28},{28,24},{32,36},... | collective-permute-start | bytes 663560 | tf_op jit(solution)/shard_map/ppermute | solution.py:20
  157.1 3.1 %fusion.20 = bf16[4,72,6,32]{1,3,2,0:T(8,128)(2,1)S(1)} fusion(bf16[4,144,6,32]{1,3,2,0:T(8,128)(2,1)S(1)} %bitcast.154, f32[4,6,72]{2,1,0:T(8,128)S(1)} %fusion.361, f32[6,72,144]{2,1,0:T(8,128)S(1)} %bitcast.147, bf16[4,144,6,32]{1,3,2,0:T(8,128)(2,1)S(1)} %bitcast.149, bf16[4,72,6,32]{3,2,0,1:T(8,128)(2,1)S(1)} %reshape_reshape.11), kind=kOutput, calls=%fused_computation.48 | convolution fusion | flops 33151824 | bytes 919296 | tf_op jit(solution)/shard_map/whqk,wkhd->wqhd/dot_general | solution.py:105
  162.3 2.4 %fusion.15 = bf16[288,192]{1,0:T(8,128)(2,1)S(1)} fusion(f32[768]{0:T(1024)S(1)} %copy-done.13, bf16[288,192]{1,0:T(8,128)(2,1)S(1)} %fusion.190, bf16[1,768,192]{2,1,0:T(8,128)(2,1)S(1)} %copy-done.1, bf16[1,192,768]{2,1,0:T(8,128)(2,1)S(1)} %copy.78, f32[192]{0:T(256)S(1)} %copy-done.24, f32[288]{0:T(512)S(1)} %add_rsqrt_fusion.3, ...), kind=kOutput, calls=%fused_computation.43 | convolution fusion | flops 185020416 | bytes 818688 | tf_op jit(solution)/shard_map/dot_general | solution.py:125
  (157 shorter events, 27.0 us)
Async XLA Ops:
  30.4 7.9 %copy-start.9 = (f32[1,1,1,6,1656]{4,2,3,1,0:T(1,128)S(1)}, f32[1,1,1,6,1656]{4,2,3,1,0:T(1,128)}, u32[]{:S(2)}) copy-start(f32[1,1,1,6,1656]{4,2,3,1,0:T(1,128)} %param.28) | copy-start | bytes 119236
  30.7 7.9 %copy-start.8 = (s32[10368]{0:T(1024)S(1)}, s32[10368]{0:T(1024)}, u32[]{:S(2)}) copy-start(s32[10368]{0:T(1024)} %constant.152) | copy-start | bytes 124420
  30.9 66.4 %collective-permute-start = (bf16[288,384]{1,0:T(8,128)(2,1)S(1)}, bf16[288,384]{1,0:T(8,128)(2,1)}, u32[]{:S(2)}, u32[]{:S(2)}) collective-permute-start(bf16[288,384]{1,0:T(8,128)(2,1)S(1)} %slice.62), channel_id=1, source_target_pairs={{0,4},{4,0},{8,12},{12,8},{16,20},{20,16},{24,28},{28,24},{32,36},... | collective-permute-start | bytes 663560 | tf_op jit(solution)/shard_map/ppermute | solution.py:20
  58.6 4.9 %copy-start.10 = (bf16[1,192,48]{1,2,0:T(8,128)(2,1)S(1)}, bf16[1,192,48]{1,2,0:T(8,128)(2,1)}, u32[]{:S(2)}) copy-start(bf16[1,192,48]{1,2,0:T(8,128)(2,1)} %param.20) | copy-start | bytes 55300
  58.6 15.2 %copy-start.7 = (bf16[1,192,192]{2,1,0:T(8,128)(2,1)S(1)}, bf16[1,192,192]{2,1,0:T(8,128)(2,1)}, u32[]{:S(2)}) copy-start(bf16[1,192,192]{2,1,0:T(8,128)(2,1)} %param.24) | copy-start | bytes 221188
  63.4 33.8 %copy-start.14 = (bf16[1,192]{1,0:T(2,128)(2,1)S(1)}, bf16[1,192]{1,0:T(2,128)(2,1)}, u32[]{:S(2)}) copy-start(bf16[1,192]{1,0:T(2,128)(2,1)} %param.22) | copy-start | bytes 1156
  63.4 33.8 %copy-start.15 = (bf16[1,192]{1,0:T(2,128)(2,1)S(1)}, bf16[1,192]{1,0:T(2,128)(2,1)}, u32[]{:S(2)}) copy-start(bf16[1,192]{1,0:T(2,128)(2,1)} %param.23) | copy-start | bytes 1156
  63.5 33.8 %copy-start = (bf16[2,2,3,48,192]{4,3,2,1,0:T(8,128)(2,1)S(1)}, bf16[2,2,3,48,192]{4,3,2,1,0:T(8,128)(2,1)}, u32[]{:S(2)}) copy-start(bf16[2,2,3,48,192]{4,3,2,1,0:T(8,128)(2,1)} %param.15) | copy-start | bytes 663556
  97.2 10.0 %copy-start.16 = (f32[1,192]{1,0:T(1,128)}, f32[1,192]{1,0:T(1,128)S(1)}, u32[]{:S(2)}) copy-start(f32[1,192]{1,0:T(1,128)S(1)} %mul.170) | copy-start | bytes 2308
  97.3 10.0 %copy-start.19 = (f32[1,192]{1,0:T(1,128)}, f32[1,192]{1,0:T(1,128)S(1)}, u32[]{:S(2)}) copy-start(f32[1,192]{1,0:T(1,128)S(1)} %add.304) | copy-start | bytes 2308
  104.4 2.9 %copy-start.1 = (bf16[1,768,192]{2,1,0:T(8,128)(2,1)S(1)}, bf16[1,768,192]{2,1,0:T(8,128)(2,1)}, u32[]{:S(2)}) copy-start(bf16[1,768,192]{2,1,0:T(8,128)(2,1)} %all_gather.30) | copy-start | bytes 884740
  104.4 2.9 %copy-start.11 = (f32[768]{0:T(1024)S(1)}, f32[768]{0:T(1024)}, u32[]{:S(2)}) copy-start(f32[768]{0:T(1024)} %add.317) | copy-start | bytes 9220
  104.4 2.9 %copy-start.22 = (f32[192]{0:T(256)S(1)}, f32[192]{0:T(256)}, u32[]{:S(2)}) copy-start(f32[192]{0:T(256)} %add.318) | copy-start | bytes 2308
  109.7 7.9 %copy-start.3 = (bf16[288,192]{1,0:T(8,128)(2,1)}, bf16[288,192]{1,0:T(8,128)(2,1)S(1)}, u32[]{:S(2)}) copy-start(bf16[288,192]{1,0:T(8,128)(2,1)S(1)} %fusion.17) | copy-start | bytes 331780
  109.7 7.4 %collective-permute-start.1 = (bf16[2,3,48,192]{3,2,1,0:T(8,128)(2,1)S(1)}, bf16[2,3,48,192]{3,2,1,0:T(8,128)(2,1)S(1)}, u32[]{:S(2)}, u32[]{:S(2)}) collective-permute-start(bf16[2,3,48,192]{3,2,1,0:T(8,128)(2,1)S(1)} %bitcast.157), channel_id=1, source_target_pairs={{0,256},{1,257},{2,258},{3,259},{4,260},{5,261},{6,262},{7,263},{8... | collective-permute-start | bytes 331784 | tf_op jit(solution)/shard_map/ppermute | solution.py:26
  118.1 11.1 %collective-permute-start.2 = (bf16[288,384]{1,0:T(8,128)(2,1)S(1)}, bf16[288,384]{1,0:T(8,128)(2,1)S(1)}, u32[]{:S(2)}, u32[]{:S(2)}) collective-permute-start(bf16[288,384]{1,0:T(8,128)(2,1)S(1)} %slice.66), channel_id=1, source_target_pairs={{0,4},{4,0},{8,12},{12,8},{16,20},{20,16},{24,28},{28,24},{32,36},... | collective-permute-start | bytes 663560 | tf_op jit(solution)/shard_map/ppermute | solution.py:20
  136.8 2.0 %copy-start.12 = (f32[768]{0:T(1024)S(1)}, f32[768]{0:T(1024)}, u32[]{:S(2)}) copy-start(f32[768]{0:T(1024)} %add.317) | copy-start | bytes 9220
  136.8 2.0 %copy-start.17 = (f32[1,192]{1,0:T(1,128)S(1)}, f32[1,192]{1,0:T(1,128)}, u32[]{:S(2)}) copy-start(f32[1,192]{1,0:T(1,128)} %copy-done.16) | copy-start | bytes 2308
  136.8 2.0 %copy-start.20 = (f32[1,192]{1,0:T(1,128)S(1)}, f32[1,192]{1,0:T(1,128)}, u32[]{:S(2)}) copy-start(f32[1,192]{1,0:T(1,128)} %copy-done.19) | copy-start | bytes 2308
  141.2 8.5 %collective-permute-start.3 = (bf16[2,3,48,192]{3,2,1,0:T(8,128)(2,1)S(1)}, bf16[2,3,48,192]{3,2,1,0:T(8,128)(2,1)S(1)}, u32[]{:S(2)}, u32[]{:S(2)}) collective-permute-start(bf16[2,3,48,192]{3,2,1,0:T(8,128)(2,1)S(1)} %bitcast.159), channel_id=1, source_target_pairs={{0,256},{1,257},{2,258},{3,259},{4,260},{5,261},{6,262},{7,263},{8... | collective-permute-start | bytes 331784 | tf_op jit(solution)/shard_map/ppermute | solution.py:26
  150.6 4.2 %collective-permute-start.4 = (bf16[288,384]{1,0:T(8,128)(2,1)S(1)}, bf16[288,384]{1,0:T(8,128)(2,1)S(1)}, u32[]{:S(2)}, u32[]{:S(2)}) collective-permute-start(bf16[288,384]{1,0:T(8,128)(2,1)S(1)} %slice.70), channel_id=1, source_target_pairs={{0,4},{4,0},{8,12},{12,8},{16,20},{20,16},{24,28},{28,24},{32,36},... | collective-permute-start | bytes 663560 | tf_op jit(solution)/shard_map/ppermute | solution.py:20
  160.3 2.0 %copy-start.13 = (f32[768]{0:T(1024)S(1)}, f32[768]{0:T(1024)}, u32[]{:S(2)}) copy-start(f32[768]{0:T(1024)} %add.317) | copy-start | bytes 9220
  162.3 2.4 %copy-start.4 = (bf16[288,192]{1,0:T(8,128)(2,1)S(1)}, bf16[288,192]{1,0:T(8,128)(2,1)}, u32[]{:S(2)}) copy-start(bf16[288,192]{1,0:T(8,128)(2,1)} %copy-done.3) | copy-start | bytes 331780
  162.3 2.4 %copy-start.6 = (bf16[288,192]{1,0:T(8,128)(2,1)S(1)}, bf16[288,192]{1,0:T(8,128)(2,1)}, u32[]{:S(2)}) copy-start(bf16[288,192]{1,0:T(8,128)(2,1)} %copy-done.5) | copy-start | bytes 331780
  (6 other events, 10.9 us)
where the time goes:
time: 166 us
  blocking collectives  50.9 us (31%)
  local copies, waits for them, and re-layouts  40.5 us (24%)
  matrix products  23.5 us (14%)
  starting transfers between devices  23 us (14%)
  waiting for transfers between devices  14 us (8%)
  other arithmetic  10.6 us (6%)
  between operations  2.91 us (2%)
    gather x2, local copies, waits for them, and re-layouts, on_device(): bias_block = jnp.take(bias_table, table_items, axis=1)  24.8 us
    ppermute x3, starting transfers between devices, swapped(): return lax.ppermute(block, axis, route)  20.3 us
    ppermute x2, waiting for transfers between devices, passed_along(): lax.ppermute(value, axis, [(source, source + steps) for source in range(f...  13.1 us
    all_gather x1, blocking collectives, on_device(): lax.all_gather(expand_weight, 'tp', axis=2, tiled=True)  12.2 us
    dot_general x3, matrix products, earth_block(): jnp.einsum('whqk,wkhd->wqhd', probs, value_heads, preferred_element_type=...  10.8 us
    all_gather x1, blocking collectives, on_device(): lax.all_gather(reduce_weight, 'tp', axis=1, tiled=True)  10.6 us
    all_gather x1, blocking collectives, on_device(): lax.all_gather(qkv_weight, 'tp', axis=2, tiled=True)  10.2 us
    all_gather x1, blocking collectives, on_device(): lax.all_gather(proj_weight, 'tp', axis=2, tiled=True)  9.17 us
  transfers between devices with their start and end apart: 5, of which 4 were waited for; matrix products, arithmetic and copies ran while one was open for 17% of the time, Pallas kernels for 0%

commit v1 on v0

--- a/solution.py
+++ b/solution.py
@@ -8,6 +8,13 @@
 WH = 6
 WW = 12
 epsilon = 1e-05
+
+
+def gather_over(shard, name, dim):
+    size = lax.axis_size(name)
+    blocks = jnp.stack([shard for _ in range(size)])
+    blocks = lax.all_to_all(blocks, name, split_axis=0, concat_axis=0)
+    return jnp.concatenate(blocks, axis=dim)
 
 
 def swapped(block, axis, apart):
@@ -145,7 +152,7 @@
     earth_bias,
 ):
     collected_values = (
-        lax.all_gather(qkv_weight, "tp", axis=2, tiled=True),
+        gather_over(qkv_weight, "tp", 2),
         lax.all_gather(qkv_bias, "tp", axis=1, tiled=True),
         lax.all_gather(proj_weight, "tp", axis=2, tiled=True),
         lax.all_gather(proj_bias, "tp", axis=1, tiled=True),

time: 166 us -> 159 us (0.958)
  the two profiles are of different devices: /device:TPU:455 before, /device:TPU:5 now
where the time goes in v1:
time: 159 us; the launch traced here: 158 us
  local copies, waits for them, and re-layouts  42.6 us (27%)
  blocking collectives  39.2 us (25%)
  starting transfers between devices  27.7 us (17%)
  matrix products  21.6 us (14%)
  waiting for transfers between devices  15.9 us (10%)
  other arithmetic  7.95 us (5%)
  between operations  2.95 us (2%)
    gather x2, local copies, waits for them, and re-layouts, on_device(): bias_block = jnp.take(bias_table, table_items, axis=1)  24.8 us
    ppermute x3, starting transfers between devices, swapped(): return lax.ppermute(block, axis, route)  20.9 us
    ppermute x2, waiting for transfers between devices, passed_along(): lax.ppermute(value, axis, [(source, source + steps) for source in range(f...  14.6 us
    all_gather x1, blocking collectives, on_device(): lax.all_gather(expand_weight, 'tp', axis=2, tiled=True)  12.8 us
    all_gather x1, blocking collectives, on_device(): lax.all_gather(reduce_weight, 'tp', axis=1, tiled=True)  10.7 us
    dot_general x3, matrix products, earth_block(): jnp.einsum('whqk,wkhd->wqhd', probs, value_heads, preferred_element_type=...  9.46 us
    all_gather x1, blocking collectives, on_device(): lax.all_gather(proj_weight, 'tp', axis=2, tiled=True)  9.04 us
    dot_general x3, matrix products, earth_block(): jnp.dot(hidden, reduce_matrix, preferred_element_type=jnp.float32)  7.16 us
  transfers between devices with their start and end apart: 6, of which 5 were waited for; matrix products, arithmetic and copies ran while one was open for 22% of the time, Pallas kernels for 0%

profile of v1, /device:TPU:5, one launch (start us, length us, event | category | flops | bytes accessed | tf_op | source)
XLA Modules:
  0.0 157.9 jit_solution(10608782921253514263)
XLA Ops:
  0.0 1.7 %stack.19 = bf16[4,1,192,144]{2,3,1,0:T(8,128)(2,1)} broadcast(bf16[192,144]{0,1:T(8,128)(2,1)} %bitcast.165), dimensions={2,3} | broadcast | bytes 276480 | tf_op jit(solution)/shard_map/stack | solution.py:15
  1.7 4.2 %all-to-all-start = ((bf16[4,1,192,144]{2,3,1,0:T(8,128)(2,1)}), bf16[4,1,192,144]{2,3,1,0:T(8,128)(2,1)S(1)}, u32[]{:S(2)}, u32[]{:S(2)}) async-start(bf16[4,1,192,144]{2,3,1,0:T(8,128)(2,1)} %stack.19), calls=%async_computation | async-start | bytes 589824 | tf_op jit(solution)/shard_map/all_to_all | solution.py:16
  11.4 12.8 %all_gather.24 = bf16[1,192,768]{1,0,2:T(2,128)(2,1)S(1)} all-gather(bf16[1,192,192]{1,0,2:T(2,128)(2,1)S(1)} %copy.78), channel_id=1, replica_groups=mesh['section'=2,'lat'=64,'tp'=4] {'tp'}, dimensions={2}, use_global_device_ids=true | all-gather | bytes 368640 | tf_op jit(solution)/shard_map/all_gather | solution.py:159
  24.2 1.3 dynamic-slice
  28.4 6.7 %all-reduce.4 = (bf16[768]{0:T(1024)(128)(2,1)S(1)}, bf16[192]{0:T(256)(128)(2,1)S(1)}, bf16[576]{0:T(1024)(128)(2,1)S(1)}, bf16[192]{0:T(256)(128)(2,1)S(1)}) all-reduce(bf16[768]{0:T(1024)(128)(2,1)S(1)} %dynamic-update-slice.2, bf16[192]{0:T(256)(128)(2,1)S(1)} %dynamic-update-slice.1, ...), channel_id=1, replica_groups=mesh['section'=2,'lat'=64,'tp'=4] {'tp'}, use_global_device_ids=true, to_apply=%add.2 | all-reduce | flops 1728 | bytes 6912
  35.5 19.9 %gather_fusion = f32[10368,6]{1,0:T(8,128)} fusion(f32[6,1656]{0,1:T(8,128)S(1)} %bitcast.127, s32[11264]{0:T(1024)S(1)} %pad_clamp_fusion), kind=kCustom, calls=%fused_computation | custom fusion | bytes 539136 | tf_op jit(solution)/shard_map/jit(_take)/gather | solution.py:171
  55.4 4.8 %copy.75 = f32[72,144,6]{1,0,2:T(8,128)S(1)} copy(f32[72,144,6]{2,1,0:T(8,128)} %bitcast.128) | data formatting | bytes 497664 | tf_op jit(solution)/shard_map/jit(_take)/gather | solution.py:171
  60.9 9.0 %all_gather.22 = bf16[1,192,192]{1,2,0:T(8,128)(2,1)S(1)} all-gather(bf16[1,192,48]{1,2,0:T(8,128)(2,1)S(1)} %copy-done.11), channel_id=1, replica_groups=mesh['section'=2,'lat'=64,'tp'=4] {'tp'}, dimensions={2}, use_global_device_ids=true | all-gather | bytes 92160 | tf_op jit(solution)/shard_map/all_gather | solution.py:157
  69.9 10.7 %all_gather.26 = bf16[1,768,192]{2,1,0:T(8,128)(2,1)} all-gather(bf16[1,192,192]{2,1,0:T(8,128)(2,1)S(1)} %copy-done.9), channel_id=1, replica_groups=mesh['section'=2,'lat'=64,'tp'=4] {'tp'}, dimensions={1}, use_global_device_ids=true | all-gather | bytes 368640 | tf_op jit(solution)/shard_map/all_gather | solution.py:161
  81.1 14.4 %collective-permute-start = (bf16[288,384]{1,0:T(8,128)(2,1)S(1)}, bf16[288,384]{1,0:T(8,128)(2,1)}, u32[]{:S(2)}, u32[]{:S(2)}) collective-permute-start(bf16[288,384]{1,0:T(8,128)(2,1)S(1)} %slice.62), channel_id=1, source_target_pairs={{0,4},{4,0},{8,12},{12,8},{16,20},{20,16},{24,28},{28,24},{32,36},... | collective-permute-start | bytes 663560 | tf_op jit(solution)/shard_map/ppermute | solution.py:27
  100.5 3.1 %fusion.18 = bf16[4,72,6,32]{1,3,2,0:T(8,128)(2,1)S(1)} fusion(bf16[4,144,6,32]{1,3,2,0:T(8,128)(2,1)S(1)} %bitcast.158, f32[4,6,72]{2,1,0:T(8,128)S(1)} %fusion.351, f32[6,72,144]{2,1,0:T(8,128)S(1)} %bitcast.146, bf16[4,144,6,32]{1,3,2,0:T(8,128)(2,1)S(1)} %bitcast.154, bf16[4,72,6,32]{3,2,0,1:T(8,128)(2,1)S(1)} %reshape_reshape.9), kind=kOutput, calls=%fused_computation.46 | convolution fusion | flops 33151824 | bytes 919296 | tf_op jit(solution)/shard_map/whqk,wkhd->wqhd/dot_general | solution.py:112
  105.6 2.4 %fusion.17 = bf16[288,192]{1,0:T(8,128)(2,1)S(1)} fusion(f32[288,192]{1,0:T(8,128)S(1)} %get-tuple-element.20, f32[768]{0:T(1024)S(1)} %add.317, bf16[1,768,192]{2,1,0:T(8,128)(2,1)S(1)} %copy-done.1, bf16[1,192,768]{2,1,0:T(8,128)(2,1)S(1)} %copy.79, f32[192]{0:T(256)S(1)} %add.318, f32[192]{0:T(256)S(1)} %bitcast.175, f32[192]{0:T(256)S(1)} %bitcast.172, ...), kind=kOutput, calls=%fused_computation.45 | convolution fusion | flops 184909824 | bytes 929280 | tf_op jit(solution)/shard_map/dot_general | solution.py:132
  108.0 1.3 collective-permute-start.1
  109.3 7.5 %collective-permute-done.1 = bf16[2,3,48,192]{3,2,1,0:T(8,128)(2,1)S(1)} collective-permute-done((bf16[2,3,48,192]{3,2,1,0:T(8,128)(2,1)S(1)}, bf16[2,3,48,192]{3,2,1,0:T(8,128)(2,1)S(1)}, u32[]{:S(2)}, u32[]{:S(2)}) %collective-permute-start.1) | collective-permute-done | bytes 110624 | tf_op jit(solution)/shard_map/ppermute | solution.py:33
  117.7 3.2 %collective-permute-start.2 = (bf16[288,384]{1,0:T(8,128)(2,1)S(1)}, bf16[288,384]{1,0:T(8,128)(2,1)}, u32[]{:S(2)}, u32[]{:S(2)}) collective-permute-start(bf16[288,384]{1,0:T(8,128)(2,1)S(1)} %slice.66), channel_id=1, source_target_pairs={{0,4},{4,0},{8,12},{12,8},{16,20},{20,16},{24,28},{28,24},{32,36},... | collective-permute-start | bytes 663560 | tf_op jit(solution)/shard_map/ppermute | solution.py:27
  124.1 1.1 fusion.355
  125.2 3.2 %fusion.19 = bf16[4,72,6,32]{1,3,2,0:T(8,128)(2,1)S(1)} fusion(bf16[4,144,6,32]{1,3,2,0:T(8,128)(2,1)S(1)} %bitcast.159, f32[4,6,72]{2,1,0:T(8,128)S(1)} %fusion.355, f32[6,72,144]{2,1,0:T(8,128)S(1)} %bitcast.148, bf16[4,144,6,32]{1,3,2,0:T(8,128)(2,1)S(1)} %bitcast.156, bf16[4,72,6,32]{3,2,0,1:T(8,128)(2,1)S(1)} %reshape_reshape.10), kind=kOutput, calls=%fused_computation.47 | convolution fusion | flops 33151824 | bytes 919296 | tf_op jit(solution)/shard_map/whqk,wkhd->wqhd/dot_general | solution.py:112
  130.3 2.4 %fusion.16 = bf16[288,192]{1,0:T(8,128)(2,1)S(1)} fusion(f32[768]{0:T(1024)S(1)} %add.317, bf16[288,192]{1,0:T(8,128)(2,1)S(1)} %fusion.186, bf16[1,768,192]{2,1,0:T(8,128)(2,1)S(1)} %copy-done.2, bf16[1,192,768]{2,1,0:T(8,128)(2,1)S(1)} %copy.79, f32[192]{0:T(256)S(1)} %add.318, f32[288]{0:T(512)S(1)} %add_rsqrt_fusion.4, ...), kind=kOutput, calls=%fused_computation.44 | convolution fusion | flops 185020416 | bytes 818688 | tf_op jit(solution)/shard_map/dot_general | solution.py:132
  132.7 1.3 collective-permute-start.3
  134.0 7.2 %collective-permute-done.3 = bf16[2,3,48,192]{3,2,1,0:T(8,128)(2,1)S(1)} collective-permute-done((bf16[2,3,48,192]{3,2,1,0:T(8,128)(2,1)S(1)}, bf16[2,3,48,192]{3,2,1,0:T(8,128)(2,1)S(1)}, u32[]{:S(2)}, u32[]{:S(2)}) %collective-permute-start.3) | collective-permute-done | bytes 110624 | tf_op jit(solution)/shard_map/ppermute | solution.py:33
  142.2 3.4 %collective-permute-start.4 = (bf16[288,384]{1,0:T(8,128)(2,1)S(1)}, bf16[288,384]{1,0:T(8,128)(2,1)S(1)}, u32[]{:S(2)}, u32[]{:S(2)}) collective-permute-start(bf16[288,384]{1,0:T(8,128)(2,1)S(1)} %slice.70), channel_id=1, source_target_pairs={{0,4},{4,0},{8,12},{12,8},{16,20},{20,16},{24,28},{28,24},{32,36},... | collective-permute-start | bytes 663560 | tf_op jit(solution)/shard_map/ppermute | solution.py:27
  148.4 1.1 fusion.358
  149.5 3.2 %fusion.20 = bf16[4,72,6,32]{1,3,2,0:T(8,128)(2,1)S(1)} fusion(bf16[4,144,6,32]{1,3,2,0:T(8,128)(2,1)S(1)} %bitcast.157, f32[4,6,72]{2,1,0:T(8,128)S(1)} %fusion.358, f32[6,72,144]{2,1,0:T(8,128)S(1)} %bitcast.150, bf16[4,144,6,32]{1,3,2,0:T(8,128)(2,1)S(1)} %bitcast.152, bf16[4,72,6,32]{3,2,0,1:T(8,128)(2,1)S(1)} %reshape_reshape.11), kind=kOutput, calls=%fused_computation.48 | convolution fusion | flops 33151824 | bytes 919296 | tf_op jit(solution)/shard_map/whqk,wkhd->wqhd/dot_general | solution.py:112
  154.7 2.4 %fusion.15 = bf16[288,192]{1,0:T(8,128)(2,1)S(1)} fusion(f32[768]{0:T(1024)S(1)} %copy-done.19, bf16[288,192]{1,0:T(8,128)(2,1)S(1)} %fusion.187, bf16[1,768,192]{2,1,0:T(8,128)(2,1)S(1)} %copy-done.2, bf16[1,192,768]{2,1,0:T(8,128)(2,1)S(1)} %copy.79, f32[192]{0:T(256)S(1)} %copy-done.31, f32[288]{0:T(512)S(1)} %add_rsqrt_fusion.3, ...), kind=kOutput, calls=%fused_computation.43 | convolution fusion | flops 185020416 | bytes 818688 | tf_op jit(solution)/shard_map/dot_general | solution.py:132
  (173 shorter events, 27.0 us)
Async XLA Ops:
  0.0 11.3 %copy-start = (bf16[2,2,3,48,192]{4,3,2,1,0:T(8,128)(2,1)S(1)}, bf16[2,2,3,48,192]{4,3,2,1,0:T(8,128)(2,1)}, u32[]{:S(2)}) copy-start(bf16[2,2,3,48,192]{4,3,2,1,0:T(8,128)(2,1)} %param.15) | copy-start | bytes 663556
  0.0 27.4 %copy-start.20 = (bf16[1,144]{1,0:T(2,128)(2,1)S(1)}, bf16[1,144]{1,0:T(2,128)(2,1)}, u32[]{:S(2)}) copy-start(bf16[1,144]{1,0:T(2,128)(2,1)} %param.19) | copy-start | bytes 868
  0.0 27.4 %copy-start.21 = (bf16[1,192]{1,0:T(2,128)(2,1)S(1)}, bf16[1,192]{1,0:T(2,128)(2,1)}, u32[]{:S(2)}) copy-start(bf16[1,192]{1,0:T(2,128)(2,1)} %param.25) | copy-start | bytes 1156
  0.0 27.5 %copy-start.28 = (bf16[1,48]{1,0:T(2,128)(2,1)S(1)}, bf16[1,48]{1,0:T(2,128)(2,1)}, u32[]{:S(2)}) copy-start(bf16[1,48]{1,0:T(2,128)(2,1)} %param.21) | copy-start | bytes 292
  0.0 27.7 %copy-start.29 = (bf16[1,48]{1,0:T(2,128)(2,1)S(1)}, bf16[1,48]{1,0:T(2,128)(2,1)}, u32[]{:S(2)}) copy-start(bf16[1,48]{1,0:T(2,128)(2,1)} %param.27) | copy-start | bytes 292
  0.0 35.1 %copy-start.10 = (f32[1,1,1,6,1656]{4,2,3,1,0:T(1,128)S(1)}, f32[1,1,1,6,1656]{4,2,3,1,0:T(1,128)}, u32[]{:S(2)}) copy-start(f32[1,1,1,6,1656]{4,2,3,1,0:T(1,128)} %param.28) | copy-start | bytes 119236
  1.7 78.9 %all-to-all-start = ((bf16[4,1,192,144]{2,3,1,0:T(8,128)(2,1)}), bf16[4,1,192,144]{2,3,1,0:T(8,128)(2,1)S(1)}, u32[]{:S(2)}, u32[]{:S(2)}) async-start(bf16[4,1,192,144]{2,3,1,0:T(8,128)(2,1)} %stack.19), calls=%async_computation | async-start | bytes 589824 | tf_op jit(solution)/shard_map/all_to_all | solution.py:16
  8.7 26.4 %copy-start.12 = (f32[1,192]{1,0:T(1,128)}, f32[1,192]{1,0:T(1,128)S(1)}, u32[]{:S(2)}) copy-start(f32[1,192]{1,0:T(1,128)S(1)} %convert_element_type.223) | copy-start | bytes 2308
  9.4 25.7 %copy-start.14 = (f32[1,192]{1,0:T(1,128)}, f32[1,192]{1,0:T(1,128)S(1)}, u32[]{:S(2)}) copy-start(f32[1,192]{1,0:T(1,128)S(1)} %convert_element_type.224) | copy-start | bytes 2308
  55.4 14.5 %copy-start.9 = (bf16[1,192,192]{2,1,0:T(8,128)(2,1)S(1)}, bf16[1,192,192]{2,1,0:T(8,128)(2,1)}, u32[]{:S(2)}) copy-start(bf16[1,192,192]{2,1,0:T(8,128)(2,1)} %param.26) | copy-start | bytes 221188
  60.3 69.4 %copy-start.16 = (f32[192]{0:T(256)}, f32[192]{0:T(256)S(1)}, u32[]{:S(2)}) copy-start(f32[192]{0:T(256)S(1)} %add.316) | copy-start | bytes 2308
  60.3 70.0 %copy-start.18 = (f32[768]{0:T(1024)}, f32[768]{0:T(1024)S(1)}, u32[]{:S(2)}) copy-start(f32[768]{0:T(1024)S(1)} %add.317) | copy-start | bytes 9220
  60.3 70.0 %copy-start.30 = (f32[192]{0:T(256)}, f32[192]{0:T(256)S(1)}, u32[]{:S(2)}) copy-start(f32[192]{0:T(256)S(1)} %add.318) | copy-start | bytes 2308
  60.8 69.5 %copy-start.24 = (f32[1,192]{1,0:T(1,128)}, f32[1,192]{1,0:T(1,128)S(1)}, u32[]{:S(2)}) copy-start(f32[1,192]{1,0:T(1,128)S(1)} %mul.170) | copy-start | bytes 2308
  60.9 69.4 %copy-start.26 = (f32[1,192]{1,0:T(1,128)}, f32[1,192]{1,0:T(1,128)S(1)}, u32[]{:S(2)}) copy-start(f32[1,192]{1,0:T(1,128)S(1)} %add.304) | copy-start | bytes 2308
  81.1 15.4 %collective-permute-start = (bf16[288,384]{1,0:T(8,128)(2,1)S(1)}, bf16[288,384]{1,0:T(8,128)(2,1)}, u32[]{:S(2)}, u32[]{:S(2)}) collective-permute-start(bf16[288,384]{1,0:T(8,128)(2,1)S(1)} %slice.62), channel_id=1, source_target_pairs={{0,4},{4,0},{8,12},{12,8},{16,20},{20,16},{24,28},{28,24},{32,36},... | collective-permute-start | bytes 663560 | tf_op jit(solution)/shard_map/ppermute | solution.py:27
  105.6 11.5 %copy-start.13 = (f32[1,192]{1,0:T(1,128)S(1)}, f32[1,192]{1,0:T(1,128)}, u32[]{:S(2)}) copy-start(f32[1,192]{1,0:T(1,128)} %copy-done.12) | copy-start | bytes 2308
  105.6 11.5 %copy-start.15 = (f32[1,192]{1,0:T(1,128)S(1)}, f32[1,192]{1,0:T(1,128)}, u32[]{:S(2)}) copy-start(f32[1,192]{1,0:T(1,128)} %copy-done.14) | copy-start | bytes 2308
  108.0 13.1 %copy-start.5 = (bf16[288,192]{1,0:T(8,128)(2,1)}, bf16[288,192]{1,0:T(8,128)(2,1)S(1)}, u32[]{:S(2)}) copy-start(bf16[288,192]{1,0:T(8,128)(2,1)S(1)} %fusion.17) | copy-start | bytes 331780
  108.0 8.8 %collective-permute-start.1 = (bf16[2,3,48,192]{3,2,1,0:T(8,128)(2,1)S(1)}, bf16[2,3,48,192]{3,2,1,0:T(8,128)(2,1)S(1)}, u32[]{:S(2)}, u32[]{:S(2)}) collective-permute-start(bf16[2,3,48,192]{3,2,1,0:T(8,128)(2,1)S(1)} %bitcast.160), channel_id=1, source_target_pairs={{0,256},{1,257},{2,258},{3,259},{4,260},{5,261},{6,262},{7,263},{8... | collective-permute-start | bytes 331784 | tf_op jit(solution)/shard_map/ppermute | solution.py:33
  117.7 4.2 %collective-permute-start.2 = (bf16[288,384]{1,0:T(8,128)(2,1)S(1)}, bf16[288,384]{1,0:T(8,128)(2,1)}, u32[]{:S(2)}, u32[]{:S(2)}) collective-permute-start(bf16[288,384]{1,0:T(8,128)(2,1)S(1)} %slice.66), channel_id=1, source_target_pairs={{0,4},{4,0},{8,12},{12,8},{16,20},{20,16},{24,28},{28,24},{32,36},... | collective-permute-start | bytes 663560 | tf_op jit(solution)/shard_map/ppermute | solution.py:27
  132.7 13.0 %copy-start.7 = (bf16[288,192]{1,0:T(8,128)(2,1)}, bf16[288,192]{1,0:T(8,128)(2,1)S(1)}, u32[]{:S(2)}) copy-start(bf16[288,192]{1,0:T(8,128)(2,1)S(1)} %fusion.16) | copy-start | bytes 331780
  132.7 8.5 %collective-permute-start.3 = (bf16[2,3,48,192]{3,2,1,0:T(8,128)(2,1)S(1)}, bf16[2,3,48,192]{3,2,1,0:T(8,128)(2,1)S(1)}, u32[]{:S(2)}, u32[]{:S(2)}) collective-permute-start(bf16[2,3,48,192]{3,2,1,0:T(8,128)(2,1)S(1)} %bitcast.162), channel_id=1, source_target_pairs={{0,256},{1,257},{2,258},{3,259},{4,260},{5,261},{6,262},{7,263},{8... | collective-permute-start | bytes 331784 | tf_op jit(solution)/shard_map/ppermute | solution.py:33
  142.2 4.2 %collective-permute-start.4 = (bf16[288,384]{1,0:T(8,128)(2,1)S(1)}, bf16[288,384]{1,0:T(8,128)(2,1)S(1)}, u32[]{:S(2)}, u32[]{:S(2)}) collective-permute-start(bf16[288,384]{1,0:T(8,128)(2,1)S(1)} %slice.70), channel_id=1, source_target_pairs={{0,4},{4,0},{8,12},{12,8},{16,20},{20,16},{24,28},{28,24},{32,36},... | collective-permute-start | bytes 663560 | tf_op jit(solution)/shard_map/ppermute | solution.py:27
  (14 other events, 36.5 us)
